TPU v7x, 32 devices: a whole 2x2x4 slice. The times are simulated.
32 devices in a mesh: dp: 8 (over y, x, core), tensor: 4 (over z).
Axes of the slice: x: 2, y: 2, z: 4, core: 2. Of those that a mesh axis runs over, the one named last changes fastest.
Arguments:
- tokens: bfloat16 [8192, 768], P(('dp', 'tensor')), may hold values from -6 to 6
- segments: int32 [8192], P('dp'), may hold values from 0 to 3, as said below
- buckets: int32 [1024], replicated, may hold values from 0 to 31, as said below
- routes: int32 [8192, 2], P(('dp', 'tensor')), may hold values from 0 to 7, all different within a row; in each aligned block of 256 rows (0 to 255, 256 to 511, ...) at most 128 rows name the same one
- norm_one: float32 [768], replicated, may hold values from 0.5 to 1.5
- w_qkv: bfloat16 [768, 3, 768], P(None, None, 'tensor'), may hold values from -0.21875 to 0.21875
- w_out: bfloat16 [768, 768], P('tensor'), may hold values from -0.625 to 0.625
- rel_bias: float32 [32, 12], P(None, 'tensor'), may hold values from -4 to 4
- norm_two: float32 [768], replicated, may hold values from 0.5 to 1.5
- w_router: bfloat16 [768, 8], replicated, may hold values from -0.21875 to 0.21875
- w_gate: bfloat16 [8, 768, 3072], P('dp', None, 'tensor'), may hold values from -0.21875 to 0.21875
- w_up: bfloat16 [8, 768, 3072], P('dp', None, 'tensor'), may hold values from -0.21875 to 0.21875
- w_down: bfloat16 [8, 3072, 768], P('dp', 'tensor'), may hold values from -0.875 to 0.875
- cotangent: bfloat16 [8192, 768], P(('dp', 'tensor')), may hold values from -6 to 6
Outputs:
- mixed_out: bfloat16 [8192, 768], P(('dp', 'tensor'))
- grad_tokens: bfloat16 [8192, 768], P(('dp', 'tensor'))
- grad_norm_one: float32 [768], replicated
- grad_qkv: float32 [768, 3, 768], P(None, None, 'tensor')
- grad_out: float32 [768, 768], P('tensor')
- grad_bias: float32 [32, 12], P(None, 'tensor')
- grad_norm_two: float32 [768], replicated
- grad_router: float32 [768, 8], replicated
- grad_gate: float32 [8, 768, 3072], P('dp', None, 'tensor')
- grad_up: float32 [8, 768, 3072], P('dp', None, 'tensor')
- grad_down: float32 [8, 3072, 768], P('dp', 'tensor')
Inputs may be any that keep to these rules, and one draw needn't show every extreme that they name: `segments`: within each block of 1024 slots of one index of dp the ids start at 0, never fall and rise by one from a sequence to the next; a sequence is a run of equal ids; in every draw some block holds a single sequence of 1024 tokens and some block four sequences. `buckets`: starts at 0, never falls, rises by at most one from a distance to the next, and ends at 31. `routes`: each row names 2 different experts; in each aligned block of 256 rows (the rows of one device) no expert is named by more than 128 rows, a bound that some block reaches.
All inputs are finite; a program needn't handle non-finite values.
Results may differ from a plain program's by a relative error of at most 0.025.
Values may be sent and summed in bfloat16 or wider, within the bound.
A program may use at most 192 MiB of HBM per device.

v0:
```python
import jax
import jax.numpy as jnp
from jax import lax
from jax.sharding import PartitionSpec as P

HD = 64
EPSILON = 1e-06
HIGHEST = lax.Precision.HIGHEST


def contract(left, right, left_dim, right_dim):
    return lax.dot_general(
        left, right, (((left_dim,), (right_dim,)), ((), ())), preferred_element_type=jnp.float32
    )


def gated(pre_gate, pre_up):
    return jax.nn.gelu(pre_gate, approximate=True) * pre_up


def carry_out(buffer):
    grouped = lax.all_gather(buffer, "tensor", axis=1, tiled=True)
    return lax.all_to_all(grouped, "dp", split_axis=0, concat_axis=0, tiled=True)


def carry_back(partial_rows):
    returned = lax.all_to_all(partial_rows, "dp", split_axis=0, concat_axis=0, tiled=True)
    return lax.psum_scatter(
        returned.astype(jnp.float32).astype(jnp.bfloat16), "tensor", scatter_dimension=1, tiled=True
    ).astype(jnp.float32)


def bucket_edges(buckets, bucket_count):
    bucket_ids = jnp.arange(bucket_count, dtype=jnp.int32)
    lower = jnp.sum((buckets[None, :] < bucket_ids[:, None]).astype(jnp.int32), axis=1)
    upper = jnp.concatenate([lower[1:], jnp.full((1,), buckets.shape[0], jnp.int32)])
    return (lower, upper)


def block_scores(query_block, key, first, segments, lower, upper, rel_bias, scale):
    count = query_block.shape[0]
    length = key.shape[0]
    distance = (first + jnp.arange(count, dtype=jnp.int32))[:, None] - jnp.arange(
        length, dtype=jnp.int32
    )[None, :]
    allowed = (distance >= 0) & (segments[first : first + count][:, None] == segments[None, :])
    reach = jnp.maximum(distance, 0)[:, :, None]
    onehot = ((reach >= lower[None, None, :]) & (reach < upper[None, None, :])).astype(jnp.float32)
    bias = jnp.einsum("ijb,bh->hij", onehot, rel_bias, precision=HIGHEST)
    scores = (
        jnp.einsum("ihd,jhd->hij", query_block, key, preferred_element_type=jnp.float32) * scale
        + bias
    )
    masked = jnp.where(allowed[None], scores, -1e30)
    return (masked, allowed, onehot)


def local(
    tokens,
    segments,
    buckets,
    routes,
    norm_one,
    w_qkv,
    w_out,
    rel_bias,
    norm_two,
    w_router,
    w_gate,
    w_up,
    w_down,
    cotangent,
):
    rows_dev = tokens.shape[0]
    width = tokens.shape[1]
    tok_dev = segments.shape[0]
    bucket_count = rel_bias.shape[0]
    heads_local = rel_bias.shape[1]
    inner = heads_local * HD
    experts = w_router.shape[1]
    groups = lax.axis_size("tensor")
    dp_count = lax.axis_size("dp")
    capacity = 4 * tok_dev // (groups * experts)
    top = routes.shape[1]
    pair_count = rows_dev * top
    block = min(512, tok_dev)
    scale = HD ** (-0.5)
    values = tokens.astype(jnp.float32)
    inverse_one = lax.rsqrt(jnp.mean(values * values, axis=1, keepdims=True) + EPSILON)
    scaled_one = values * inverse_one
    normed_one = (scaled_one * norm_one).astype(jnp.bfloat16)
    normed_all = lax.all_gather(normed_one, "tensor", axis=0, tiled=True)
    proj_weight = w_qkv.reshape(width, 3 * inner)
    projected = jnp.dot(normed_all, proj_weight, preferred_element_type=jnp.float32).astype(
        jnp.bfloat16
    )
    query = projected[:, :inner].reshape(tok_dev, heads_local, HD)
    key = projected[:, inner : 2 * inner].reshape(tok_dev, heads_local, HD)
    value = projected[:, 2 * inner :].reshape(tok_dev, heads_local, HD)
    lower, upper = bucket_edges(buckets, bucket_count)
    contexts = []
    logsums = []
    for first in range(0, tok_dev, block):
        masked, allowed, onehot = block_scores(
            query[first : first + block], key, first, segments, lower, upper, rel_bias, scale
        )
        peak = jnp.max(masked, axis=2, keepdims=True)
        logsum = peak + jnp.log(jnp.sum(jnp.exp(masked - peak), axis=2, keepdims=True))
        probs = jnp.where(allowed[None], jnp.exp(masked - logsum), 0.0)
        probs_low = probs.astype(jnp.bfloat16)
        context_block = jnp.einsum(
            "hij,jhd->ihd", probs_low, value, preferred_element_type=jnp.float32
        )
        contexts.append(context_block.astype(jnp.bfloat16).reshape(block, inner))
        logsums.append(logsum)
    context = jnp.concatenate(contexts, axis=0)
    rows = context
    attended = lax.psum_scatter(
        jnp.dot(rows, w_out, preferred_element_type=jnp.float32).astype(jnp.bfloat16),
        "tensor",
        scatter_dimension=0,
        tiled=True,
    ).astype(jnp.float32)
    hidden = values + attended
    inverse_two = lax.rsqrt(jnp.mean(hidden * hidden, axis=1, keepdims=True) + EPSILON)
    scaled_two = hidden * inverse_two
    normed_two = (scaled_two * norm_two).astype(jnp.bfloat16)
    logits = jnp.dot(normed_two, w_router, preferred_element_type=jnp.float32)
    router = jax.nn.softmax(logits, axis=1)
    choose = (routes[:, :, None] == jnp.arange(experts, dtype=jnp.int32)[None, None, :]).astype(
        jnp.float32
    )
    gate_vals = jnp.sum(choose * router[:, None, :], axis=2)
    expert_ids = routes.reshape(-1)
    member = (expert_ids[:, None] == jnp.arange(experts, dtype=jnp.int32)[None, :]).astype(
        jnp.int32
    )
    earlier = jnp.cumsum(member, axis=0) - member
    place = jnp.sum(earlier * member, axis=1)
    slot = expert_ids * capacity + place
    owner = (
        jnp.full((experts * capacity,), -1, dtype=jnp.int32)
        .at[slot]
        .set(jnp.arange(pair_count, dtype=jnp.int32))
    )
    filled = (owner >= 0)[:, None]
    owner_pair = jnp.maximum(owner, 0)
    send_rows = jnp.where(filled, normed_two[owner_pair // top], 0).reshape(
        experts, capacity, width
    )
    rows_in = carry_out(send_rows).reshape(-1, width)
    gate_weight = w_gate[0]
    up_weight = w_up[0]
    down_weight = w_down[0]
    pre_gate = jnp.dot(rows_in, gate_weight, preferred_element_type=jnp.float32)
    pre_up = jnp.dot(rows_in, up_weight, preferred_element_type=jnp.float32)
    active = gated(pre_gate, pre_up).astype(jnp.bfloat16)
    partial_rows = jnp.dot(active, down_weight, preferred_element_type=jnp.float32).astype(
        jnp.bfloat16
    )
    back_slots = carry_back(partial_rows.reshape(dp_count, groups * capacity, width)).reshape(
        experts * capacity, width
    )
    pair_out = back_slots[slot].reshape(rows_dev, top, width)
    mixed = hidden + jnp.sum(gate_vals[:, :, None] * pair_out, axis=1)
    upstream = cotangent.astype(jnp.float32)
    grad_gates = jnp.sum(upstream[:, None, :] * pair_out, axis=2)
    grad_pairs = (
        (gate_vals[:, :, None] * upstream[:, None, :])
        .astype(jnp.bfloat16)
        .reshape(pair_count, width)
    )
    send_grads = jnp.where(filled, grad_pairs[owner_pair], 0).reshape(experts, capacity, width)
    grad_in = carry_out(send_grads).reshape(-1, width)
    grad_active = contract(grad_in, down_weight, 1, 1)
    grad_down = contract(active, grad_in, 0, 0)
    unused, pull = jax.vjp(gated, pre_gate, pre_up)
    grad_pre_gate, grad_pre_up = pull(grad_active)
    grad_pre_gate = grad_pre_gate.astype(jnp.bfloat16)
    grad_pre_up = grad_pre_up.astype(jnp.bfloat16)
    grad_gate = contract(rows_in, grad_pre_gate, 0, 0)
    grad_up = contract(rows_in, grad_pre_up, 0, 0)
    grad_rows_x = (
        contract(grad_pre_gate, gate_weight, 1, 1) + contract(grad_pre_up, up_weight, 1, 1)
    ).astype(jnp.bfloat16)
    grad_slots = carry_back(grad_rows_x.reshape(dp_count, groups * capacity, width)).reshape(
        experts * capacity, width
    )
    grad_pair_rows = grad_slots[slot].reshape(rows_dev, top, width)
    grad_router_probs = jnp.sum(choose * grad_gates[:, :, None], axis=1)
    grad_logits = (
        router * (grad_router_probs - jnp.sum(router * grad_router_probs, axis=1, keepdims=True))
    ).astype(jnp.bfloat16)
    grad_router = contract(normed_two, grad_logits, 0, 0)
    grad_normed_two = jnp.sum(grad_pair_rows, axis=1) + contract(grad_logits, w_router, 1, 1)
    grad_norm_two = jnp.sum(grad_normed_two * scaled_two, axis=0)
    spread_two = grad_normed_two * norm_two
    grad_hidden = upstream + inverse_two * (
        spread_two - scaled_two * jnp.mean(spread_two * scaled_two, axis=1, keepdims=True)
    )
    grad_attended = grad_hidden.astype(jnp.bfloat16)
    piece = lax.all_gather(grad_attended, "tensor", axis=0, tiled=True)
    rows = context
    grad_out_sum = contract(rows, piece, 0, 0)
    grad_piece = contract(piece, w_out, 1, 1)
    grad_context_all = grad_piece
    grad_out_local, grad_context_all = (grad_out_sum, grad_context_all)
    grad_context = grad_context_all.astype(jnp.bfloat16).reshape(tok_dev, heads_local, HD)
    query_grads = []
    grad_key = jnp.zeros((tok_dev, heads_local, HD), jnp.float32)
    grad_value = jnp.zeros((tok_dev, heads_local, HD), jnp.float32)
    grad_bias_local = jnp.zeros((bucket_count, heads_local), jnp.float32)
    for index, first in enumerate(range(0, tok_dev, block)):
        masked, allowed, onehot = block_scores(
            query[first : first + block], key, first, segments, lower, upper, rel_bias, scale
        )
        probs = jnp.where(allowed[None], jnp.exp(masked - logsums[index]), 0.0)
        probs_low = probs.astype(jnp.bfloat16)
        grad_block = grad_context[first : first + block]
        grad_probs = jnp.einsum(
            "ihd,jhd->hij", grad_block, value, preferred_element_type=jnp.float32
        )
        row_delta = jnp.sum(probs * grad_probs, axis=2, keepdims=True)
        grad_scores = (probs * (grad_probs - row_delta)).astype(jnp.bfloat16)
        query_grads.append(
            jnp.einsum("hij,jhd->ihd", grad_scores, key, preferred_element_type=jnp.float32) * scale
        )
        grad_key = (
            grad_key
            + jnp.einsum(
                "hij,ihd->jhd",
                grad_scores,
                query[first : first + block],
                preferred_element_type=jnp.float32,
            )
            * scale
        )
        grad_value = grad_value + jnp.einsum(
            "hij,ihd->jhd", probs_low, grad_block, preferred_element_type=jnp.float32
        )
        grad_bias_local = grad_bias_local + jnp.einsum(
            "hij,ijb->bh", grad_scores.astype(jnp.float32), onehot, precision=HIGHEST
        )
    grad_query = jnp.concatenate(query_grads, axis=0)
    grad_proj_rows = jnp.concatenate(
        [
            grad_query.reshape(tok_dev, inner),
            grad_key.reshape(tok_dev, inner),
            grad_value.reshape(tok_dev, inner),
        ],
        axis=1,
    ).astype(jnp.bfloat16)
    grad_qkv_local = contract(normed_all, grad_proj_rows, 0, 0).reshape(width, 3, inner)
    rows = grad_proj_rows
    grad_normed_one = lax.psum_scatter(
        contract(rows, proj_weight, 1, 1).astype(jnp.bfloat16),
        "tensor",
        scatter_dimension=0,
        tiled=True,
    ).astype(jnp.float32)
    grad_norm_one = jnp.sum(grad_normed_one * scaled_one, axis=0)
    spread_one = grad_normed_one * norm_one
    grad_tokens = grad_hidden + inverse_one * (
        spread_one - scaled_one * jnp.mean(spread_one * scaled_one, axis=1, keepdims=True)
    )
    grad_qkv_sum, grad_out_sum, grad_bias_sum = lax.psum(
        (grad_qkv_local, grad_out_local, grad_bias_local), "dp"
    )
    grad_router_sum, grad_two_sum, grad_one_sum = lax.psum(
        (grad_router, grad_norm_two, grad_norm_one), ("dp", "tensor")
    )
    return (
        mixed.astype(jnp.bfloat16),
        grad_tokens.astype(jnp.bfloat16),
        grad_one_sum,
        grad_qkv_sum,
        grad_out_sum,
        grad_bias_sum,
        grad_two_sum,
        grad_router_sum,
        grad_gate[None],
        grad_up[None],
        grad_down[None],
    )


def solution(mesh):
    return jax.shard_map(
        local,
        mesh=mesh,
        in_specs=(
            P(("dp", "tensor"), None),
            P("dp"),
            P(),
            P(("dp", "tensor"), None),
            P(),
            P(None, None, "tensor"),
            P("tensor", None),
            P(None, "tensor"),
            P(),
            P(),
            P("dp", None, "tensor"),
            P("dp", None, "tensor"),
            P("dp", "tensor", None),
            P(("dp", "tensor"), None),
        ),
        out_specs=(
            P(("dp", "tensor"), None),
            P(("dp", "tensor"), None),
            P(),
            P(None, None, "tensor"),
            P("tensor", None),
            P(None, "tensor"),
            P(),
            P(),
            P("dp", None, "tensor"),
            P("dp", None, "tensor"),
            P("dp", "tensor", None),
        ),
        check_vma=False,
    )
```

profile of v0, /device:TPU:0, one launch (start us, length us, event | category | flops | bytes accessed | tf_op | source)
XLA Modules:
  0.0 987.0 jit_solution(7135961302743151335)
XLA Ops:
  12.3 25.9 %fusion.3 = f32[512,1024,3]{1,2,0:T(4,128)} fusion(s32[512,1024]{1,0:T(8,128)S(1)} %fusion.29, s32[32]{0:T(128)S(1)} %pad_add_fusion, s32[32]{0:T(128)S(1)} %convert_reduce_fusion, f32[32,3]{0,1:T(4,128)} %param.21), kind=kOutput, calls=%fused_computation.10 | convolution fusion | flops 654311424 | bytes 8389248 | tf_op jit(solution)/shard_map/ijb,bh->hij/dot_general | solution.py:49
  40.0 25.4 %fusion.1 = f32[512,1024,3]{1,2,0:T(4,128)} fusion(s32[512,1024]{1,0:T(8,128)S(1)} %fusion.31, s32[32]{0:T(128)S(1)} %pad_add_fusion, s32[32]{0:T(128)S(1)} %convert_reduce_fusion, f32[32,3]{0,1:T(4,128)S(1)} %copy-done.60), kind=kOutput, calls=%fused_computation.8 | convolution fusion | flops 654311424 | bytes 8389248 | tf_op jit(solution)/shard_map/ijb,bh->hij/dot_general | solution.py:49
  68.1 8.4 fusion.105
  100.2 28.7 %reduce-scatter.5.cloned.1.call-done = bf16[256,768]{1,0:T(8,128)(2,1)} async-done(((bf16[1024,768]{1,0:T(8,128)(2,1)}), bf16[256,768]{1,0:T(8,128)(2,1)}) %reduce-scatter.5.cloned.1.call-update) | async-done | bytes 393232 | tf_op jit(solution)/shard_map/reduce_scatter | solution.py:118
  148.4 113.8 %all-gather.7.cloned.1.call-done = bf16[8,512,768]{2,1,0:T(8,128)(2,1)} async-done(((bf16[8,128,768]{2,1,0:T(8,128)(2,1)}), bf16[8,512,768]{2,1,0:T(8,128)(2,1)}) %all-gather.7.cloned.1.call-update) | async-done | bytes 6291472 | tf_op jit(solution)/shard_map/all_gather | solution.py:22
  267.1 110.7 %all-gather.9.cloned.1.call-done = bf16[8,512,768]{2,1,0:T(8,128)(2,1)} async-done(((bf16[8,128,768]{2,1,0:T(8,128)(2,1)}), bf16[8,512,768]{2,1,0:T(8,128)(2,1)}) %all-gather.9.cloned.1.call-update) | async-done | bytes 6291472 | tf_op jit(solution)/shard_map/all_gather | solution.py:22
  382.6 10.4 %fusion.46 = f32[4096,768]{1,0:T(8,128)} fusion(bf16[4096,768]{1,0:T(8,128)(2,1)} %bitcast.18, bf16[1,768,768]{2,1,0:T(8,128)(2,1)} %param.25), kind=kOutput, calls=%fused_computation.95 | convolution fusion | flops 4831838208 | bytes 20054016 | tf_op jit(solution)/shard_map/dot_general | solution.py:156
  393.0 10.5 %fusion.50 = f32[4096,768]{1,0:T(8,128)} fusion(bf16[4096,768]{1,0:T(8,128)(2,1)} %bitcast.18, bf16[1,768,768]{2,1,0:T(8,128)(2,1)S(1)} %copy-done.56), kind=kOutput, calls=%fused_computation.99 | convolution fusion | flops 4831838208 | bytes 20054016 | tf_op jit(solution)/shard_map/dot_general | solution.py:155
  403.5 50.6 %all-to-all-done.2 = bf16[8,512,768]{2,1,0:T(8,128)(2,1)} async-done(((bf16[8,512,768]{2,1,0:T(8,128)(2,1)}), bf16[8,512,768]{2,1,0:T(8,128)(2,1)}, u32[]{:S(2)}, u32[]{:S(2)}) %all-to-all-start.2) | async-done | bytes 6291488 | tf_op jit(solution)/shard_map/all_to_all | solution.py:23
  454.2 21.3 %multiply_convert_fusion = (bf16[4096,768]{1,0:T(8,128)(2,1)}, bf16[4096,768]{1,0:T(8,128)(2,1)}, bf16[4096,768]{1,0:T(8,128)(2,1)S(1)}) fusion(f32[4096,768]{1,0:T(8,128)} %fusion.50, f32[4096,768]{1,0:T(8,128)} %fusion.46, bf16[4096,768]{1,0:T(8,128)(2,1)} %bitcast.25, bf16[1,768,768]{2,1,0:T(8,128)(2,1)S(1)} %copy-done), kind=kOutput, calls=%fused_computation.33 | convolution fusion | flops 4913627136 | bytes 51511296 | tf_op jit(solution)/shard_map/dot_general | solution.py:12
  480.7 74.9 %all_to_all.20 = bf16[8,512,768]{2,1,0:T(8,128)(2,1)} all-to-all(bf16[8,512,768]{2,1,0:T(8,128)(2,1)S(1)} %bitcast.146), channel_id=1, replica_groups=mesh['dp'=8,'tensor'=4] {'dp'}, dimensions={0} | all-to-all | bytes 12582912 | tf_op jit(solution)/shard_map/all_to_all | solution.py:27
  555.7 11.8 %fusion.48 = f32[4096,768]{1,0:T(8,128)} fusion(bf16[4096,768]{1,0:T(8,128)(2,1)} %get-tuple-element.23, bf16[1,768,768]{2,1,0:T(8,128)(2,1)S(1)} %copy-done.56), kind=kOutput, calls=%fused_computation.97 | convolution fusion | flops 4831838208 | bytes 20054016 | tf_op jit(solution)/shard_map/dot_general | solution.py:12
  567.5 10.1 %add_convert_fusion = bf16[4096,768]{1,0:T(8,128)(2,1)S(1)} fusion(f32[4096,768]{1,0:T(8,128)} %fusion.48, bf16[4096,768]{1,0:T(8,128)(2,1)} %get-tuple-element.22, bf16[1,768,768]{2,1,0:T(8,128)(2,1)S(1)} %copy-done.57), kind=kOutput, calls=%fused_computation.32 | convolution fusion | flops 4838129664 | bytes 26345472 | tf_op jit(solution)/shard_map/dot_general | solution.py:12
  577.6 74.9 %all_to_all.21 = bf16[8,512,768]{2,1,0:T(8,128)(2,1)} all-to-all(bf16[8,512,768]{2,1,0:T(8,128)(2,1)S(1)} %bitcast.145), channel_id=1, replica_groups=mesh['dp'=8,'tensor'=4] {'dp'}, dimensions={0} | all-to-all | bytes 12582912 | tf_op jit(solution)/shard_map/all_to_all | solution.py:27
  652.7 10.3 %reduce-scatter.7.cloned.1.call-done = bf16[8,128,768]{2,1,0:T(8,128)(2,1)} async-done(((bf16[8,512,768]{2,1,0:T(8,128)(2,1)}), bf16[8,128,768]{2,1,0:T(8,128)(2,1)}) %reduce-scatter.7.cloned.1.call-update) | async-done | bytes 1572880 | tf_op jit(solution)/shard_map/reduce_scatter | solution.py:28
  679.8 96.7 %reduce-scatter.9.cloned.1.call-done = bf16[8,128,768]{2,1,0:T(8,128)(2,1)} async-done(((bf16[8,512,768]{2,1,0:T(8,128)(2,1)}), bf16[8,128,768]{2,1,0:T(8,128)(2,1)}) %reduce-scatter.9.cloned.1.call-update) | async-done | bytes 1572880 | tf_op jit(solution)/shard_map/reduce_scatter | solution.py:28
  793.0 10.2 %convolution_bitcast_fusion = f32[1,768,768]{2,1,0:T(8,128)} fusion(bf16[4096,768]{1,0:T(8,128)(2,1)} %copy-done.63, bf16[4096,768]{1,0:T(8,128)(2,1)} %bitcast.25), kind=kOutput, calls=%fused_computation.62 | convolution fusion | flops 4831838208 | bytes 14942208 | tf_op jit(solution)/shard_map/dot_general | solution.py:12
  803.2 10.1 %convolution_bitcast_fusion.1 = f32[1,768,768]{2,1,0:T(8,128)} fusion(bf16[4096,768]{1,0:T(8,128)(2,1)} %bitcast.18, bf16[4096,768]{1,0:T(8,128)(2,1)} %get-tuple-element.22), kind=kOutput, calls=%fused_computation.63 | convolution fusion | flops 4831838208 | bytes 14942208 | tf_op jit(solution)/shard_map/dot_general | solution.py:12
  813.3 17.3 %all-gather.11.cloned.1.call-done = bf16[1024,768]{1,0:T(8,128)(2,1)} async-done(((bf16[256,768]{1,0:T(8,128)(2,1)}), bf16[1024,768]{1,0:T(8,128)(2,1)}) %all-gather.11.cloned.1.call-update) | async-done | bytes 1572880 | tf_op jit(solution)/shard_map/all_gather | solution.py:202
  867.7 10.5 %convolution_bitcast_fusion.2 = f32[1,768,768]{2,1,0:T(8,128)} fusion(bf16[4096,768]{1,0:T(8,128)(2,1)} %bitcast.18, bf16[4096,768]{1,0:T(8,128)(2,1)} %get-tuple-element.23), kind=kOutput, calls=%fused_computation.64 | convolution fusion | flops 4831838208 | bytes 14942208 | tf_op jit(solution)/shard_map/dot_general | solution.py:12
  882.9 17.2 %fusion.56 = f32[32,3]{0,1:T(4,128)S(1)} fusion(bf16[3,512,1024]{2,1,0:T(8,128)(2,1)S(1)} %copy-done.7, s32[512,1024]{1,0:T(8,128)S(1)} %copy-done.26, s32[32]{0:T(128)S(1)} %copy-done.62, s32[32]{0:T(128)S(1)} %copy-done.54), kind=kOutput, calls=%fused_computation.107 | convolution fusion | flops 150994944 | bytes 5243520 | tf_op jit(solution)/shard_map/hij,ijb->bh/dot_general | solution.py:241
  900.2 17.7 %fusion.62 = f32[32,3]{0,1:T(4,128)S(1)} fusion(f32[32,3]{0,1:T(4,128)S(1)} %fusion.56, bf16[3,512,1024]{2,1,0:T(8,128)(2,1)} %get-tuple-element.53, s32[512,1024]{1,0:T(8,128)} %copy-done.27, s32[32]{0:T(128)S(1)} %copy-done.62, s32[32]{0:T(128)S(1)} %copy-done.54), kind=kOutput, calls=%fused_computation.109 | convolution fusion | flops 150995040 | bytes 5243904 | tf_op jit(solution)/shard_map/hij,ijb->bh/dot_general | solution.py:241
  917.9 14.2 %psum.45 = f32[32,3]{0,1:T(4,128)} all-reduce(f32[32,3]{0,1:T(4,128)S(1)} %fusion.62), channel_id=1, replica_groups=mesh['dp'=8,'tensor'=4] {'dp'}, use_global_device_ids=true, to_apply=%region_31.32 | all-reduce | flops 96 | bytes 768 | tf_op jit(solution)/shard_map/psum | solution.py:266
  933.5 39.2 %all-reduce = (f32[768]{0:T(1024)}, f32[768]{0:T(1024)}, f32[768,8]{0,1:T(8,128)}) all-reduce(f32[768]{0:T(1024)S(1)} %get-tuple-element.15, f32[768]{0:T(1024)S(1)} %get-tuple-element.11, f32[768,8]{0,1:T(8,128)S(1)} %fusion.109), channel_id=1, replica_groups=mesh['dp'=8,'tensor'=4] {'dp','tensor'}, use_global_device_ids=true, to_apply=%region_28.29 | all-reduce | flops 7680 | bytes 61440 | tf_op jit(solution)/shard_map/psum | solution.py:269
  (260 shorter events, 150.7 us)
Async XLA Ops:
  7.2 447.0 %copy-start = (bf16[1,768,768]{2,1,0:T(8,128)(2,1)S(1)}, bf16[1,768,768]{2,1,0:T(8,128)(2,1)}, u32[]{:S(2)}) copy-start(bf16[1,768,768]{2,1,0:T(8,128)(2,1)} %param.26) | copy-start | bytes 3538948
  7.2 58.2 %all-gather.5.cloned.1.call-start = ((), (), s32[]{:S(2)}) async-start(), calls=%async_computation.8 | async-start | bytes 1966080 | tf_op jit(solution)/shard_map/all_gather | solution.py:92
  11.0 117.9 %reduce-scatter.5.cloned.1.call-start = ((), (), s32[]{:S(2)}) async-start(), calls=%async_computation.9 | async-start | bytes 1966080 | tf_op jit(solution)/shard_map/reduce_scatter | solution.py:118
  39.9 45.1 %copy-start.8 = (pred[512,1024]{1,0:T(8,128)(4,1)}, pred[512,1024]{1,0:T(8,128)(4,1)S(1)}, u32[]{:S(2)}) copy-start(pred[512,1024]{1,0:T(8,128)(4,1)S(1)} %get-tuple-element.36) | copy-start | bytes 1572868
  39.9 46.7 %copy-start.10 = (pred[512,1024]{1,0:T(8,128)(4,1)}, pred[512,1024]{1,0:T(8,128)(4,1)S(1)}, u32[]{:S(2)}) copy-start(pred[512,1024]{1,0:T(8,128)(4,1)S(1)} %get-tuple-element.35) | copy-start | bytes 1572868
  88.2 40.7 %copy-start.12 = (bf16[256,768]{1,0:T(8,128)(2,1)S(1)}, bf16[256,768]{1,0:T(8,128)(2,1)}, u32[]{:S(2)}) copy-start(bf16[256,768]{1,0:T(8,128)(2,1)} %param.14) | copy-start | bytes 1179652
  88.2 41.9 %copy-start.46 = (f32[768]{0:T(1024)S(1)}, f32[768]{0:T(1024)}, u32[]{:S(2)}) copy-start(f32[768]{0:T(1024)} %param.22) | copy-start | bytes 9220
  88.2 43.1 %copy-start.47 = (bf16[768,8]{0,1:T(8,128)(2,1)S(1)}, bf16[768,8]{0,1:T(8,128)(2,1)}, u32[]{:S(2)}) copy-start(bf16[768,8]{0,1:T(8,128)(2,1)} %param.23) | copy-start | bytes 36868
  90.7 171.5 %all-gather.7.cloned.1.call-start = ((), (), s32[]{:S(2)}) async-start(), calls=%async_computation.10 | async-start | bytes 7864320 | tf_op jit(solution)/shard_map/all_gather | solution.py:22
  147.8 230.0 %all-gather.9.cloned.1.call-start = ((), (), s32[]{:S(2)}) async-start(), calls=%async_computation.12 | async-start | bytes 7864320 | tf_op jit(solution)/shard_map/all_gather | solution.py:22
  262.2 115.6 %all-to-all-start = ((bf16[8,512,768]{2,1,0:T(8,128)(2,1)}), bf16[8,512,768]{2,1,0:T(8,128)(2,1)}, u32[]{:S(2)}, u32[]{:S(2)}) async-start(bf16[8,512,768]{2,1,0:T(8,128)(2,1)} %all-gather.7.cloned.1.call-done), calls=%async_computation.1 | async-start | bytes 12582912 | tf_op jit(solution)/shard_map/all_to_all | solution.py:23
  377.8 76.4 %all-to-all-start.2 = ((bf16[8,512,768]{2,1,0:T(8,128)(2,1)}), bf16[8,512,768]{2,1,0:T(8,128)(2,1)}, u32[]{:S(2)}, u32[]{:S(2)}) async-start(bf16[8,512,768]{2,1,0:T(8,128)(2,1)} %all-gather.9.cloned.1.call-done), calls=%async_computation.4 | async-start | bytes 12582912 | tf_op jit(solution)/shard_map/all_to_all | solution.py:23
  382.6 280.4 %reduce-scatter.7.cloned.1.call-start = ((), (), s32[]{:S(2)}) async-start(), calls=%async_computation.11 | async-start | bytes 7864320 | tf_op jit(solution)/shard_map/reduce_scatter | solution.py:28
  555.7 220.8 %reduce-scatter.9.cloned.1.call-start = ((), (), s32[]{:S(2)}) async-start(), calls=%async_computation.13 | async-start | bytes 7864320 | tf_op jit(solution)/shard_map/reduce_scatter | solution.py:28
  652.5 178.1 %all-gather.11.cloned.1.call-start = ((), (), s32[]{:S(2)}) async-start(), calls=%async_computation.14 | async-start | bytes 1966080 | tf_op jit(solution)/shard_map/all_gather | solution.py:202
  792.9 139.2 %reduce-scatter.11.cloned.1.call-start = ((), (), s32[]{:S(2)}) async-start(), calls=%async_computation.15 | async-start | bytes 1966080 | tf_op jit(solution)/shard_map/reduce_scatter | solution.py:255
  803.2 29.6 %copy-start.22 = (bf16[1024,192]{0,1:T(8,128)(2,1)S(1)}, bf16[1024,192]{0,1:T(8,128)(2,1)}, u32[]{:S(2)}) copy-start(bf16[1024,192]{0,1:T(8,128)(2,1)} %copy-done.21) | copy-start | bytes 1179652
  803.2 29.6 %copy-start.45 = (f32[3,512]{1,0:T(4,128)S(1)}, f32[3,512]{1,0:T(4,128)}, u32[]{:S(2)}) copy-start(f32[3,512]{1,0:T(4,128)} %copy-done.44) | copy-start | bytes 18436
  867.7 107.7 %all-reduce.4.cloned.1.call-start = ((), (), s32[]{:S(2)}) async-start(), calls=%async_computation.16 | async-start | bytes 4718592 | tf_op jit(solution)/shard_map/psum | solution.py:266
  900.2 31.9 %copy-start.48 = (f32[768]{0:T(1024)S(1)}, f32[768]{0:T(1024)}, u32[]{:S(2)}) copy-start(f32[768]{0:T(1024)} %param.18) | copy-start | bytes 9220
  900.2 31.9 %copy-start.51 = (f32[256]{0:T(256)S(1)}, f32[256]{0:T(256)}, u32[]{:S(2)}) copy-start(f32[256]{0:T(256)} %copy-done.50) | copy-start | bytes 3076
  900.2 72.5 %copy-start.17 = (f32[256,768]{1,0:T(8,128)S(1)}, f32[256,768]{1,0:T(8,128)}, u32[]{:S(2)}) copy-start(f32[256,768]{1,0:T(8,128)} %copy-done.16) | copy-start | bytes 2359300
  900.2 72.5 %copy-start.20 = (bf16[256,768]{1,0:T(8,128)(2,1)S(1)}, bf16[256,768]{1,0:T(8,128)(2,1)}, u32[]{:S(2)}) copy-start(bf16[256,768]{1,0:T(8,128)(2,1)} %param.27) | copy-start | bytes 1179652
  900.2 79.9 %copy-start.1 = (bf16[1,768,768]{2,1,0:T(8,128)(2,1)S(1)}, bf16[1,768,768]{2,1,0:T(8,128)(2,1)}, u32[]{:S(2)}) copy-start(bf16[1,768,768]{2,1,0:T(8,128)(2,1)} %param.26) | copy-start | bytes 3538948
  (57 other events, 547.2 us)
Sparse Core Ops, SparseCore 0:
  11.1 39.7 all-gather.4
  90.8 38.0 reduce-scatter.4
  147.9 114.2 all-gather.6
  264.2 113.5 all-gather.8
  555.8 107.1 reduce-scatter.6
  665.1 111.2 reduce-scatter.8
  793.0 37.6 all-gather.10
  867.7 34.1 reduce-scatter.10
  905.8 62.1 all-reduce.3
where the time goes:
time: 996 us; the launch traced here: 987 us
  waiting for transfers between devices  429 us (43%)
  matrix products  241 us (24%)
  blocking collectives  203 us (20%)
  other arithmetic  46.1 us (5%)
  local copies, waits for them, and re-layouts  42.7 us (4%)
  between operations  15.4 us (2%)
  starting transfers between devices  9.99 us (1%)
    all_gather x2, waiting for transfers between devices, carry_out(): grouped = lax.all_gather(buffer, 'tensor', axis=1, tiled=True)  225 us
    all_to_all x2, blocking collectives, carry_back(): lax.all_to_all(partial_rows, 'dp', split_axis=0, concat_axis=0, tiled=True)  150 us
    reduce_scatter x2, waiting for transfers between devices, carry_back(): lax.psum_scatter(returned.astype(jnp.float32).astype(jnp.bfloat16), 'tens...  107 us
    dot_general x12, matrix products, contract(): lax.dot_general(left, right, (((left_dim,), (right_dim,)), ((), ())), pre...  82.9 us
    dot_general x2, matrix products, block_scores(): bias = jnp.einsum('ijb,bh->hij', onehot, rel_bias, precision=HIGHEST)  51.3 us
    all_to_all x2, waiting for transfers between devices, carry_out(): lax.all_to_all(grouped, 'dp', split_axis=0, concat_axis=0, tiled=True)  50.6 us
    psum x1, blocking collectives, local(): lax.psum((grad_router, grad_norm_two, grad_norm_one), ('dp', 'tensor'))  39.2 us
    dot_general x2, matrix products, local(): jnp.einsum('hij,ijb->bh', grad_scores.astype(jnp.float32), onehot, precis...  34.9 us
  transfers between devices with their start and end apart: 11, of which 7 were waited for; matrix products, arithmetic and copies ran while one was open for 20% of the time, Pallas kernels for 0%

commit v1 on v0

--- a/solution.py
+++ b/solution.py
@@ -19,7 +19,14 @@
 
 
 def carry_out(buffer):
-    grouped = lax.all_gather(buffer, "tensor", axis=1, tiled=True)
+    ways, here = (lax.axis_size("tensor"), lax.axis_index("tensor"))
+    grouped, reach_2 = (buffer, 1)
+    while reach_2 < ways:
+        theirs = lax.ppermute(grouped, "tensor", [(d, d ^ reach_2) for d in range(ways)])
+        mine_first = jnp.concatenate([grouped, theirs], axis=1)
+        theirs_first = jnp.concatenate([theirs, grouped], axis=1)
+        grouped = jnp.where(here & reach_2 == 0, mine_first, theirs_first)
+        reach_2 = 2 * reach_2
     return lax.all_to_all(grouped, "dp", split_axis=0, concat_axis=0, tiled=True)
 
 

time: 996 us -> 1110 us (1.11)
  waiting for transfers between devices: 429 us -> 515 us
  other arithmetic: 46.1 us -> 67.7 us
    ppermute x0 -> x4, waiting for transfers between devices: none -> 309 us  [carry_out(): lax.ppermute(grouped, 'tensor', [(d, d ^ reach_2) for d in range(ways)])]
    all_gather x2 -> x0, waiting for transfers between devices: 225 us -> none  [carry_out(): grouped = lax.all_gather(buffer, 'tensor', axis=1, tiled=True)]
    select_n x0 -> x4, other arithmetic: none -> 21.6 us  [carry_out(): grouped = jnp.where(here & reach_2 == 0, mine_first, theirs_first)]
  transfers between devices with their start and end apart: 11 -> 13, of which waited for: 7 -> 8; matrix products, arithmetic and copies ran while one was open for 20% -> 19% of each run, Pallas kernels for 0% -> 0%
where the time goes in v1:
time: 1110 us; the launch traced here: 1100 us
  waiting for transfers between devices  515 us (46%)
  matrix products  239 us (22%)
  blocking collectives  203 us (18%)
  other arithmetic  67.7 us (6%)
  local copies, waits for them, and re-layouts  42.7 us (4%)
  between operations  15.7 us (1%)
  starting transfers between devices  13.1 us (1%)
    ppermute x4, waiting for transfers between devices, carry_out(): lax.ppermute(grouped, 'tensor', [(d, d ^ reach_2) for d in range(ways)])  309 us
    all_to_all x2, blocking collectives, carry_back(): lax.all_to_all(partial_rows, 'dp', split_axis=0, concat_axis=0, tiled=True)  150 us
    reduce_scatter x2, waiting for transfers between devices, carry_back(): lax.psum_scatter(returned.astype(jnp.float32).astype(jnp.bfloat16), 'tens...  109 us
    dot_general x12, matrix products, contract(): lax.dot_general(left, right, (((left_dim,), (right_dim,)), ((), ())), pre...  81.6 us
    dot_general x2, matrix products, block_scores(): bias = jnp.einsum('ijb,bh->hij', onehot, rel_bias, precision=HIGHEST)  51.3 us
    all_to_all x2, waiting for transfers between devices, carry_out(): lax.all_to_all(grouped, 'dp', split_axis=0, concat_axis=0, tiled=True)  50.7 us
    psum x1, blocking collectives, local(): lax.psum((grad_router, grad_norm_two, grad_norm_one), ('dp', 'tensor'))  39.2 us
    dot_general x2, matrix products, local(): jnp.einsum('hij,ijb->bh', grad_scores.astype(jnp.float32), onehot, precis...  34.9 us
  transfers between devices with their start and end apart: 13, of which 8 were waited for; matrix products, arithmetic and copies ran while one was open for 19% of the time, Pallas kernels for 0%

profile of v1, /device:TPU:0, one launch (start us, length us, event | category | flops | bytes accessed | tf_op | source)
XLA Modules:
  0.0 1096.5 jit_solution(9813510297868350629)
XLA Ops:
  12.3 25.9 %fusion.3 = f32[512,1024,3]{1,2,0:T(4,128)} fusion(s32[512,1024]{1,0:T(8,128)S(1)} %fusion.29, s32[32]{0:T(128)S(1)} %pad_add_fusion, s32[32]{0:T(128)S(1)} %convert_reduce_fusion, f32[32,3]{0,1:T(4,128)} %param.21), kind=kOutput, calls=%fused_computation.10 | convolution fusion | flops 654311424 | bytes 8389248 | tf_op jit(solution)/shard_map/ijb,bh->hij/dot_general | solution.py:56
  39.9 25.4 %fusion.1 = f32[512,1024,3]{1,2,0:T(4,128)} fusion(s32[512,1024]{1,0:T(8,128)S(1)} %fusion.31, s32[32]{0:T(128)S(1)} %pad_add_fusion, s32[32]{0:T(128)S(1)} %convert_reduce_fusion, f32[32,3]{0,1:T(4,128)S(1)} %copy-done.60), kind=kOutput, calls=%fused_computation.8 | convolution fusion | flops 654311424 | bytes 8389248 | tf_op jit(solution)/shard_map/ijb,bh->hij/dot_general | solution.py:56
  100.1 28.7 %reduce-scatter.5.cloned.1.call-done = bf16[256,768]{1,0:T(8,128)(2,1)} async-done(((bf16[1024,768]{1,0:T(8,128)(2,1)}), bf16[256,768]{1,0:T(8,128)(2,1)}) %reduce-scatter.5.cloned.1.call-update) | async-done | bytes 393232 | tf_op jit(solution)/shard_map/reduce_scatter | solution.py:125
  148.0 35.9 %collective-permute-done = bf16[8,128,768]{2,1,0:T(8,128)(2,1)} collective-permute-done((bf16[8,128,768]{2,1,0:T(8,128)(2,1)}, bf16[8,128,768]{2,1,0:T(8,128)(2,1)}, u32[]{:S(2)}, u32[]{:S(2)}) %collective-permute-start) | collective-permute-done | bytes 1572896 | tf_op jit(solution)/shard_map/ppermute | solution.py:25
  191.0 134.9 %collective-permute-done.1 = bf16[8,256,768]{2,1,0:T(8,128)(2,1)} collective-permute-done((bf16[8,256,768]{2,1,0:T(8,128)(2,1)}, bf16[8,256,768]{2,1,0:T(8,128)(2,1)}, u32[]{:S(2)}, u32[]{:S(2)}) %collective-permute-start.1) | collective-permute-done | bytes 3145760 | tf_op jit(solution)/shard_map/ppermute | solution.py:25
  343.4 138.1 %collective-permute-done.3 = bf16[8,256,768]{2,1,0:T(8,128)(2,1)S(1)} collective-permute-done((bf16[8,256,768]{2,1,0:T(8,128)(2,1)S(1)}, bf16[8,256,768]{2,1,0:T(8,128)(2,1)S(1)}, u32[]{:S(2)}, u32[]{:S(2)}) %collective-permute-start.3) | collective-permute-done | bytes 3145760 | tf_op jit(solution)/shard_map/ppermute | solution.py:25
  490.6 10.2 fusion.46
  500.9 10.5 fusion.50
  511.4 50.7 %all-to-all-done.2 = bf16[8,512,768]{2,1,0:T(8,128)(2,1)} async-done(((bf16[8,512,768]{2,1,0:T(8,128)(2,1)}), bf16[8,512,768]{2,1,0:T(8,128)(2,1)}, u32[]{:S(2)}, u32[]{:S(2)}) %all-to-all-start.2) | async-done | bytes 6291488 | tf_op jit(solution)/shard_map/all_to_all | solution.py:30
  562.2 21.4 %multiply_convert_fusion = (bf16[4096,768]{1,0:T(8,128)(2,1)}, bf16[4096,768]{1,0:T(8,128)(2,1)}, bf16[4096,768]{1,0:T(8,128)(2,1)S(1)}) fusion(f32[4096,768]{1,0:T(8,128)} %fusion.50, f32[4096,768]{1,0:T(8,128)} %fusion.46, bf16[4096,768]{1,0:T(8,128)(2,1)} %bitcast.25, bf16[1,768,768]{2,1,0:T(8,128)(2,1)S(1)} %copy-done), kind=kOutput, calls=%fused_computation.33 | convolution fusion | flops 4913627136 | bytes 51511296 | tf_op jit(solution)/shard_map/dot_general | solution.py:12
  588.8 74.9 %all_to_all.20 = bf16[8,512,768]{2,1,0:T(8,128)(2,1)} all-to-all(bf16[8,512,768]{2,1,0:T(8,128)(2,1)S(1)} %bitcast.146), channel_id=1, replica_groups=mesh['dp'=8,'tensor'=4] {'dp'}, dimensions={0} | all-to-all | bytes 12582912 | tf_op jit(solution)/shard_map/all_to_all | solution.py:34
  664.2 10.7 fusion.48
  675.0 10.0 add_convert_fusion
  684.9 74.9 %all_to_all.21 = bf16[8,512,768]{2,1,0:T(8,128)(2,1)} all-to-all(bf16[8,512,768]{2,1,0:T(8,128)(2,1)S(1)} %bitcast.145), channel_id=1, replica_groups=mesh['dp'=8,'tensor'=4] {'dp'}, dimensions={0} | all-to-all | bytes 12582912 | tf_op jit(solution)/shard_map/all_to_all | solution.py:34
  760.0 12.2 %reduce-scatter.7.cloned.1.call-done = bf16[8,128,768]{2,1,0:T(8,128)(2,1)} async-done(((bf16[8,512,768]{2,1,0:T(8,128)(2,1)}), bf16[8,128,768]{2,1,0:T(8,128)(2,1)}) %reduce-scatter.7.cloned.1.call-update) | async-done | bytes 1572880 | tf_op jit(solution)/shard_map/reduce_scatter | solution.py:35
  789.0 96.6 %reduce-scatter.9.cloned.1.call-done = bf16[8,128,768]{2,1,0:T(8,128)(2,1)} async-done(((bf16[8,512,768]{2,1,0:T(8,128)(2,1)}), bf16[8,128,768]{2,1,0:T(8,128)(2,1)}) %reduce-scatter.9.cloned.1.call-update) | async-done | bytes 1572880 | tf_op jit(solution)/shard_map/reduce_scatter | solution.py:35
  902.3 10.1 convolution_bitcast_fusion
  912.4 10.1 convolution_bitcast_fusion.1
  922.5 17.3 %all-gather.5.cloned.1.call-done = bf16[1024,768]{1,0:T(8,128)(2,1)} async-done(((bf16[256,768]{1,0:T(8,128)(2,1)}), bf16[1024,768]{1,0:T(8,128)(2,1)}) %all-gather.5.cloned.1.call-update) | async-done | bytes 1572880 | tf_op jit(solution)/shard_map/all_gather | solution.py:209
  976.9 10.5 convolution_bitcast_fusion.2
  992.1 17.2 %fusion.56 = f32[32,3]{0,1:T(4,128)S(1)} fusion(bf16[3,512,1024]{2,1,0:T(8,128)(2,1)S(1)} %copy-done.7, s32[512,1024]{1,0:T(8,128)S(1)} %copy-done.26, s32[32]{0:T(128)S(1)} %copy-done.62, s32[32]{0:T(128)S(1)} %copy-done.54), kind=kOutput, calls=%fused_computation.111 | convolution fusion | flops 150994944 | bytes 5243520 | tf_op jit(solution)/shard_map/hij,ijb->bh/dot_general | solution.py:248
  1009.4 17.7 %fusion.62 = f32[32,3]{0,1:T(4,128)S(1)} fusion(f32[32,3]{0,1:T(4,128)S(1)} %fusion.56, bf16[3,512,1024]{2,1,0:T(8,128)(2,1)} %get-tuple-element.53, s32[512,1024]{1,0:T(8,128)} %copy-done.27, s32[32]{0:T(128)S(1)} %copy-done.62, s32[32]{0:T(128)S(1)} %copy-done.54), kind=kOutput, calls=%fused_computation.113 | convolution fusion | flops 150995040 | bytes 5243904 | tf_op jit(solution)/shard_map/hij,ijb->bh/dot_general | solution.py:248
  1027.1 14.2 %psum.45 = f32[32,3]{0,1:T(4,128)} all-reduce(f32[32,3]{0,1:T(4,128)S(1)} %fusion.62), channel_id=1, replica_groups=mesh['dp'=8,'tensor'=4] {'dp'}, use_global_device_ids=true, to_apply=%region_31.32 | all-reduce | flops 96 | bytes 768 | tf_op jit(solution)/shard_map/psum | solution.py:273
  1042.6 39.2 %all-reduce = (f32[768]{0:T(1024)}, f32[768]{0:T(1024)}, f32[768,8]{0,1:T(8,128)}) all-reduce(f32[768]{0:T(1024)S(1)} %get-tuple-element.15, f32[768]{0:T(1024)S(1)} %get-tuple-element.11, f32[768,8]{0,1:T(8,128)S(1)} %fusion.109), channel_id=1, replica_groups=mesh['dp'=8,'tensor'=4] {'dp','tensor'}, use_global_device_ids=true, to_apply=%region_28.29 | all-reduce | flops 7680 | bytes 61440 | tf_op jit(solution)/shard_map/psum | solution.py:276
  (266 shorter events, 183.3 us)
Async XLA Ops:
  7.2 555.0 %copy-start = (bf16[1,768,768]{2,1,0:T(8,128)(2,1)S(1)}, bf16[1,768,768]{2,1,0:T(8,128)(2,1)}, u32[]{:S(2)}) copy-start(bf16[1,768,768]{2,1,0:T(8,128)(2,1)} %param.26) | copy-start | bytes 3538948
  7.2 58.2 %all-gather.3.cloned.1.call-start = ((), (), s32[]{:S(2)}) async-start(), calls=%async_computation.8 | async-start | bytes 1966080 | tf_op jit(solution)/shard_map/all_gather | solution.py:99
  11.0 117.9 %reduce-scatter.5.cloned.1.call-start = ((), (), s32[]{:S(2)}) async-start(), calls=%async_computation.9 | async-start | bytes 1966080 | tf_op jit(solution)/shard_map/reduce_scatter | solution.py:125
  39.9 45.2 %copy-start.8 = (pred[512,1024]{1,0:T(8,128)(4,1)}, pred[512,1024]{1,0:T(8,128)(4,1)S(1)}, u32[]{:S(2)}) copy-start(pred[512,1024]{1,0:T(8,128)(4,1)S(1)} %get-tuple-element.36) | copy-start | bytes 1572868
  39.9 46.7 %copy-start.10 = (pred[512,1024]{1,0:T(8,128)(4,1)}, pred[512,1024]{1,0:T(8,128)(4,1)S(1)}, u32[]{:S(2)}) copy-start(pred[512,1024]{1,0:T(8,128)(4,1)S(1)} %get-tuple-element.35) | copy-start | bytes 1572868
  88.2 40.6 %copy-start.12 = (bf16[256,768]{1,0:T(8,128)(2,1)S(1)}, bf16[256,768]{1,0:T(8,128)(2,1)}, u32[]{:S(2)}) copy-start(bf16[256,768]{1,0:T(8,128)(2,1)} %param.14) | copy-start | bytes 1179652
  88.2 41.8 %copy-start.46 = (f32[768]{0:T(1024)S(1)}, f32[768]{0:T(1024)}, u32[]{:S(2)}) copy-start(f32[768]{0:T(1024)} %param.22) | copy-start | bytes 9220
  88.2 43.0 %copy-start.47 = (bf16[768,8]{0,1:T(8,128)(2,1)S(1)}, bf16[768,8]{0,1:T(8,128)(2,1)}, u32[]{:S(2)}) copy-start(bf16[768,8]{0,1:T(8,128)(2,1)} %param.23) | copy-start | bytes 36868
  147.7 36.3 %collective-permute-start = (bf16[8,128,768]{2,1,0:T(8,128)(2,1)}, bf16[8,128,768]{2,1,0:T(8,128)(2,1)}, u32[]{:S(2)}, u32[]{:S(2)}) collective-permute-start(bf16[8,128,768]{2,1,0:T(8,128)(2,1)} %get-tuple-element.40), channel_id=1, source_target_pairs={{0,1},{1,0},{2,3},{3,2},{4,5},{5,4},{6,7},{7,6},{8,9},{9,8},{10,11... | collective-permute-start | bytes 4718600 | tf_op jit(solution)/shard_map/ppermute | solution.py:25
  188.9 137.0 %collective-permute-start.1 = (bf16[8,256,768]{2,1,0:T(8,128)(2,1)}, bf16[8,256,768]{2,1,0:T(8,128)(2,1)}, u32[]{:S(2)}, u32[]{:S(2)}) collective-permute-start(bf16[8,256,768]{2,1,0:T(8,128)(2,1)} %maximum_select_fusion.2), channel_id=1, source_target_pairs={{0,2},{1,3},{2,0},{3,1},{4,6},{5,7},{6,4},{7,5},{8,10},{9,11},{10,... | collective-permute-start | bytes 9437192 | tf_op jit(solution)/shard_map/ppermute | solution.py:25
  190.5 149.1 %collective-permute-start.2 = (bf16[8,128,768]{2,1,0:T(8,128)(2,1)}, bf16[8,128,768]{2,1,0:T(8,128)(2,1)}, u32[]{:S(2)}, u32[]{:S(2)}) collective-permute-start(bf16[8,128,768]{2,1,0:T(8,128)(2,1)} %get-tuple-element.39), channel_id=1, source_target_pairs={{0,1},{1,0},{2,3},{3,2},{4,5},{5,4},{6,7},{7,6},{8,9},{9,8},{10,11... | collective-permute-start | bytes 4718600 | tf_op jit(solution)/shard_map/ppermute | solution.py:25
  334.9 150.7 %all-to-all-start = ((bf16[8,512,768]{2,1,0:T(8,128)(2,1)}), bf16[8,512,768]{2,1,0:T(8,128)(2,1)}, u32[]{:S(2)}, u32[]{:S(2)}) async-start(bf16[8,512,768]{2,1,0:T(8,128)(2,1)} %maximum_select_fusion), calls=%async_computation.1 | async-start | bytes 12582912 | tf_op jit(solution)/shard_map/all_to_all | solution.py:30
  343.3 138.2 %collective-permute-start.3 = (bf16[8,256,768]{2,1,0:T(8,128)(2,1)S(1)}, bf16[8,256,768]{2,1,0:T(8,128)(2,1)S(1)}, u32[]{:S(2)}, u32[]{:S(2)}) collective-permute-start(bf16[8,256,768]{2,1,0:T(8,128)(2,1)S(1)} %maximum_select_fusion.3), channel_id=1, source_target_pairs={{0,2},{1,3},{2,0},{3,1},{4,6},{5,7},{6,4},{7,5},{8,10},{9,11},{10,... | collective-permute-start | bytes 9437192 | tf_op jit(solution)/shard_map/ppermute | solution.py:25
  485.6 76.6 %all-to-all-start.2 = ((bf16[8,512,768]{2,1,0:T(8,128)(2,1)}), bf16[8,512,768]{2,1,0:T(8,128)(2,1)}, u32[]{:S(2)}, u32[]{:S(2)}) async-start(bf16[8,512,768]{2,1,0:T(8,128)(2,1)} %maximum_select_fusion.1), calls=%async_computation.4 | async-start | bytes 12582912 | tf_op jit(solution)/shard_map/all_to_all | solution.py:30
  490.6 281.6 %reduce-scatter.7.cloned.1.call-start = ((), (), s32[]{:S(2)}) async-start(), calls=%async_computation.10 | async-start | bytes 7864320 | tf_op jit(solution)/shard_map/reduce_scatter | solution.py:35
  663.8 221.8 %reduce-scatter.9.cloned.1.call-start = ((), (), s32[]{:S(2)}) async-start(), calls=%async_computation.11 | async-start | bytes 7864320 | tf_op jit(solution)/shard_map/reduce_scatter | solution.py:35
  759.9 180.0 %all-gather.5.cloned.1.call-start = ((), (), s32[]{:S(2)}) async-start(), calls=%async_computation.12 | async-start | bytes 1966080 | tf_op jit(solution)/shard_map/all_gather | solution.py:209
  902.1 139.2 %reduce-scatter.11.cloned.1.call-start = ((), (), s32[]{:S(2)}) async-start(), calls=%async_computation.13 | async-start | bytes 1966080 | tf_op jit(solution)/shard_map/reduce_scatter | solution.py:262
  976.8 107.7 %all-reduce.4.cloned.1.call-start = ((), (), s32[]{:S(2)}) async-start(), calls=%async_computation.14 | async-start | bytes 4718592 | tf_op jit(solution)/shard_map/psum | solution.py:273
  1009.3 31.9 %copy-start.48 = (f32[768]{0:T(1024)S(1)}, f32[768]{0:T(1024)}, u32[]{:S(2)}) copy-start(f32[768]{0:T(1024)} %param.18) | copy-start | bytes 9220
  1009.3 31.9 %copy-start.51 = (f32[256]{0:T(256)S(1)}, f32[256]{0:T(256)}, u32[]{:S(2)}) copy-start(f32[256]{0:T(256)} %copy-done.50) | copy-start | bytes 3076
  1009.4 72.5 %copy-start.17 = (f32[256,768]{1,0:T(8,128)S(1)}, f32[256,768]{1,0:T(8,128)}, u32[]{:S(2)}) copy-start(f32[256,768]{1,0:T(8,128)} %copy-done.16) | copy-start | bytes 2359300
  1009.4 72.4 %copy-start.20 = (bf16[256,768]{1,0:T(8,128)(2,1)S(1)}, bf16[256,768]{1,0:T(8,128)(2,1)}, u32[]{:S(2)}) copy-start(bf16[256,768]{1,0:T(8,128)(2,1)} %param.27) | copy-start | bytes 1179652
  1009.4 79.9 %copy-start.1 = (bf16[1,768,768]{2,1,0:T(8,128)(2,1)S(1)}, bf16[1,768,768]{2,1,0:T(8,128)(2,1)}, u32[]{:S(2)}) copy-start(bf16[1,768,768]{2,1,0:T(8,128)(2,1)} %param.26) | copy-start | bytes 3538948
  (59 other events, 605.3 us)
Sparse Core Ops, SparseCore 0:
  11.1 39.7 all-gather.2
  90.8 37.9 reduce-scatter.4
  663.9 108.2 reduce-scatter.6
  774.3 111.2 reduce-scatter.8
  902.2 37.6 all-gather.4
  976.9 34.1 reduce-scatter.10
  1015.0 62.1 all-reduce.3
